TPU v7x, 256 devices: a whole 4x4x8 slice. The times are simulated.
256 devices in a mesh: expert: 32 (over z, x), col: 8 (over y, core).
Axes of the slice: x: 4, y: 4, z: 8, core: 2. Of those that a mesh axis runs over, the one named last changes fastest.
Arguments:
- tokens: bfloat16 [4096, 4096], P('expert', 'col'), may hold values from -6 to 6
- routes: int32 [4096, 8], P('expert'), may hold values from 0 to 63, all different within a row; in each aligned block of 128 rows (0 to 127, 128 to 255, ...) at most 24 rows name the same one
- route_weight: float32 [4096, 8], P('expert'), may hold values from 0.02 to 0.25
- language: int32 [4096], P('expert'), may hold values from 0 to 118
- lang_weight: float32 [119], replicated, may hold values from 0.01 to 0.1
- w_gate: bfloat16 [64, 1536, 4096], P('expert', 'col'), may hold values from -0.09375 to 0.09375
- w_up: bfloat16 [64, 1536, 4096], P('expert', 'col'), may hold values from -0.09375 to 0.09375
- w_down: bfloat16 [64, 1536, 4096], P('expert', None, 'col'), may hold values from -0.15625 to 0.15625
Outputs:
- layer_out: bfloat16 [4096, 4096], P('expert', 'col')
- gram: float32 [64, 1536, 1536], P('expert', 'col')
Inputs may be any that keep to these rules, and one draw needn't show every extreme that they name: `routes`: each row names 8 different experts. In each aligned block of 128 rows no expert is named by more than 24 rows, a bound that some block reaches.
All inputs are finite; a program needn't handle non-finite values.
Results may differ from a plain program's by a relative error of at most 0.0063.
Values may be sent and summed in bfloat16 or wider, within the bound.
A program may use at most 128 MiB of HBM per device.

v0:
```python
import jax
import jax.numpy as jnp
from jax import lax
from jax.sharding import PartitionSpec as P


def on_device(tokens, routes, route_weight, language, lang_weight, w_gate, w_up, w_down):
    tok_rows = routes.shape[0]
    top_count = routes.shape[1]
    local_exp = w_gate.shape[0]
    owners = lax.axis_size("expert")
    experts = local_exp * owners
    capacity = tok_rows * top_count * 3 // (2 * experts)
    expert_ids = jnp.arange(experts, dtype=jnp.int32)
    chosen = routes[:, :, None] == expert_ids[None, None, :]
    hits = jnp.any(chosen, axis=1).astype(jnp.int32)
    coefs = jnp.sum(jnp.where(chosen, route_weight[:, :, None], jnp.zeros((), jnp.float32)), axis=1)
    places = jnp.cumsum(hits, axis=0) - hits
    slot_ids = jnp.arange(capacity, dtype=jnp.int32)
    picks = (hits.T[:, None, :] == 1) & (places.T[:, None, :] == slot_ids[None, :, None])
    row_index = jnp.arange(tok_rows, dtype=jnp.int32)
    slot_token = jnp.sum(jnp.where(picks, row_index[None, None, :], 0), axis=2)
    filled = jnp.any(picks, axis=2)
    lang_table = language[:, None] == jnp.arange(lang_weight.shape[0], dtype=jnp.int32)[None, :]
    calib = jnp.sum(
        jnp.where(lang_table, lang_weight[None, :], jnp.zeros((), jnp.float32)), axis=1
    ).astype(jnp.bfloat16)
    slot_cal = jnp.where(filled, calib[slot_token], jnp.zeros((), jnp.bfloat16)).reshape(
        owners, local_exp, capacity
    )
    slot_coef = jnp.where(
        filled, jnp.take_along_axis(coefs.T, slot_token, axis=1), jnp.zeros((), jnp.float32)
    )
    flat_token = slot_token.reshape(-1)
    flat_filled = filled.reshape(-1)
    whole = lax.all_gather(tokens, "col", axis=1, tiled=True)
    rows = jnp.take(whole, flat_token, axis=0)
    rows = jnp.where(flat_filled[:, None], rows, jnp.zeros((), jnp.bfloat16))
    arrived = lax.all_to_all(
        rows.reshape(owners, local_exp, capacity, whole.shape[1]),
        "expert",
        split_axis=0,
        concat_axis=0,
        tiled=True,
    )
    arrived_cal = lax.all_to_all(slot_cal, "expert", split_axis=0, concat_axis=0, tiled=True)
    gate = jnp.einsum("seck,efk->escf", arrived, w_gate, preferred_element_type=jnp.float32)
    upper = jnp.einsum("seck,efk->escf", arrived, w_up, preferred_element_type=jnp.float32)
    hidden = (jax.nn.silu(gate) * upper).astype(jnp.bfloat16)
    cal_rows = jnp.transpose(arrived_cal, (1, 0, 2))
    scaled = (cal_rows[..., None].astype(jnp.float32) * hidden.astype(jnp.float32)).astype(
        jnp.bfloat16
    )
    d_local = w_down.shape[2]
    piece = lax.all_gather(hidden, "col", axis=3, tiled=True)
    block = jnp.einsum("escu,escv->euv", scaled, piece, preferred_element_type=jnp.float32)
    mixed_now = jnp.einsum("escv,evd->escd", piece, w_down, preferred_element_type=jnp.float32)
    expert_out = mixed_now.astype(jnp.bfloat16)
    returned = lax.all_to_all(expert_out, "expert", split_axis=1, concat_axis=0, tiled=True)
    returned = returned.reshape(experts * capacity, d_local).astype(jnp.float32)
    combined = jnp.zeros((tok_rows, d_local), jnp.float32)
    combined = combined.at[flat_token].add(slot_coef.reshape(-1)[:, None] * returned)
    return (combined.astype(jnp.bfloat16), block)


def solution(mesh):
    in_specs = (
        P("expert", "col"),
        P("expert", None),
        P("expert", None),
        P("expert"),
        P(),
        P("expert", "col", None),
        P("expert", "col", None),
        P("expert", None, "col"),
    )
    out_specs = (P("expert", "col"), P("expert", "col", None))
    return jax.shard_map(
        on_device, mesh=mesh, in_specs=in_specs, out_specs=out_specs, check_vma=False
    )
```

profile of v0, /device:TPU:4, one launch (start us, length us, event | category | flops | bytes accessed | tf_op | source)
XLA Modules:
  0.0 570.8 jit_solution(8276990550696766480)
XLA Ops:
  7.2 0.7 all-gather.3.cloned.1.call-update
  8.0 0.9 fusion.18
  9.3 1.2 select_reduce_fusion
  10.6 1.2 fusion.17
  11.9 26.8 %all-gather.3.cloned.1.call-done = bf16[128,4096]{1,0:T(8,128)(2,1)} async-done(((bf16[128,512]{1,0:T(8,128)(2,1)}), bf16[128,4096]{1,0:T(8,128)(2,1)}) %all-gather.3.cloned.1.call-update) | async-done | bytes 1048592 | tf_op jit(solution)/shard_map/all_gather | solution.py:36
  38.8 23.4 %gather_fusion = bf16[1536,4096]{1,0:T(8,128)(2,1)} fusion(bf16[128,4096]{1,0:T(8,128)(2,1)} %all-gather.3.cloned.1.call-done, s32[2048]{0:T(1024)S(1)} %pad_clamp_fusion.1), kind=kCustom, calls=%fused_computation | custom fusion | bytes 25171968 | tf_op jit(solution)/shard_map/jit(_take)/gather | solution.py:37
  62.2 6.7 %select_select_fusion = bf16[32,2,24,4096]{3,2,1,0:T(8,128)(2,1)S(1)} fusion(bf16[32,2,24,4096]{3,2,1,0:T(8,128)(2,1)} %bitcast.49, pred[32,2,24]{2,1,0:T(4,128)(4,1)S(1)} %compare_and_fusion, pred[32,2,24]{2,1,0:T(4,128)(4,1)S(1)} %broadcast_in_dim.95), kind=kLoop, calls=%fused_computation.4 | loop fusion | flops 12582912 | bytes 25168896 | tf_op jit(solution)/shard_map/jit(_where)/select_n | solution.py:38
  68.9 285.7 %all_to_all.19 = bf16[32,2,24,4096]{3,2,1,0:T(8,128)(2,1)} all-to-all(bf16[32,2,24,4096]{3,2,1,0:T(8,128)(2,1)S(1)} %select_select_fusion), channel_id=1, replica_groups=mesh['expert'=32,'col'=8] {'expert'}, dimensions={0} | all-to-all | bytes 25165824 | tf_op jit(solution)/shard_map/all_to_all | solution.py:39
  354.6 10.1 %fusion.2 = f32[2,32,24,192]{3,2,1,0:T(8,128)} fusion(bf16[32,2,24,4096]{3,2,1,0:T(8,128)(2,1)} %all_to_all.19, bf16[2,192,4096]{2,1,0:T(8,128)(2,1)} %param.13), kind=kOutput, calls=%fused_computation.7 | convolution fusion | flops 2415919104 | bytes 16908288 | tf_op jit(solution)/shard_map/seck,efk->escf/dot_general | solution.py:47
  364.7 10.5 %multiply_convert_fusion.1 = bf16[2,32,24,192]{3,2,1,0:T(8,128)(2,1)} fusion(f32[2,32,24,192]{3,2,1,0:T(8,128)} %fusion.2, bf16[2,192,4096]{2,1,0:T(8,128)(2,1)} %param.14, bf16[32,2,24,4096]{3,2,1,0:T(8,128)(2,1)} %all_to_all.19), kind=kOutput, calls=%fused_computation.18 | convolution fusion | flops 2417688576 | bytes 17498112 | tf_op jit(solution)/shard_map/seck,efk->escf/dot_general | solution.py:48
  375.1 3.7 copy.44
  379.1 9.0 %gather_fusion.1 = bf16[1536]{0:T(1024)(128)(2,1)S(1)} fusion(bf16[128]{0:T(256)(128)(2,1)S(1)} %select_reduce_fusion.2, s32[2048]{0:T(1024)S(1)} %pad_clamp_fusion), kind=kCustom, calls=%fused_computation.1 | custom fusion | bytes 12288 | tf_op jit(solution)/shard_map/gather | solution.py:28
  388.8 5.5 all-to-all-start.2
  394.4 76.2 %all-gather.5.cloned.1.call-done = bf16[2,32,24,1536]{1,2,0,3:T(8,128)(2,1)} async-done(((bf16[2,32,24,192]{1,2,0,3:T(8,128)(2,1)}), bf16[2,32,24,1536]{1,2,0,3:T(8,128)(2,1)}) %all-gather.5.cloned.1.call-update) | async-done | bytes 4718608 | tf_op jit(solution)/shard_map/all_gather | solution.py:55
  470.6 22.1 %copy.45 = bf16[2,32,24,1536]{3,2,1,0:T(8,128)(2,1)} copy(bf16[2,32,24,1536]{1,2,0,3:T(8,128)(2,1)} %all-gather.5.cloned.1.call-done) | data formatting | bytes 9437184 | tf_op jit(solution)/shard_map/all_gather | solution.py:55
  492.7 5.0 fusion.8
  497.8 1.3 copy.46
  499.1 10.2 %all-to-all-start.1 = ((bf16[2,32,24,512]{3,2,0,1:T(8,128)(2,1)}), bf16[2,32,24,512]{3,2,0,1:T(8,128)(2,1)}, u32[]{:S(2)}, u32[]{:S(2)}) async-start(bf16[2,32,24,512]{3,2,0,1:T(8,128)(2,1)} %copy.46), calls=%async_computation.1 | async-start | bytes 3145728 | tf_op jit(solution)/shard_map/all_to_all | solution.py:59
  509.7 10.7 %gather_fusion.2 = f32[1536]{0:T(1024)S(1)} fusion(f32[64,128]{0,1:T(8,128)S(1)} %bitcast.48, s32[1536]{0:T(1024)S(1)} %reshape.137), kind=kCustom, calls=%fused_computation.2 | custom fusion | bytes 24576 | tf_op jit(solution)/shard_map/jit(take_along_axis)/gather | solution.py:32
  520.5 5.2 convolution_bitcast_fusion
  525.6 23.4 %all-to-all-done.1 = bf16[2,32,24,512]{3,2,0,1:T(8,128)(2,1)} async-done(((bf16[2,32,24,512]{3,2,0,1:T(8,128)(2,1)}), bf16[2,32,24,512]{3,2,0,1:T(8,128)(2,1)}, u32[]{:S(2)}, u32[]{:S(2)}) %all-to-all-start.1) | async-done | bytes 1572896 | tf_op jit(solution)/shard_map/all_to_all | solution.py:59
  549.1 1.8 bitcast_convert_fusion
  550.9 1.9 bitcast_multiply_fusion
  552.8 10.4 %scatter_custom_fusion = f32[128,512]{1,0:T(8,128)S(1)} fusion(s32[1536]{0:T(1024)S(1)} %fusion.21, f32[1536,512]{1,0:T(8,128)} %bitcast_multiply_fusion, f32[]{:T(128)} %constant.16.clone.1), kind=kCustom, calls=%fused_computation.27 | custom fusion | flops 786432 | bytes 262656 | tf_op jit(solution)/shard_map/scatter-add | solution.py:62
  (40 shorter events, 2.8 us)
Async XLA Ops:
  7.2 485.5 %copy-start = (bf16[2,1536,512]{2,1,0:T(8,128)(2,1)S(1)}, bf16[2,1536,512]{2,1,0:T(8,128)(2,1)}, u32[]{:S(2)}) copy-start(bf16[2,1536,512]{2,1,0:T(8,128)(2,1)} %param.15) | copy-start | bytes 9437188
  7.2 31.6 %all-gather.3.cloned.1.call-start = ((), (), s32[]{:S(2)}) async-start(), calls=%async_computation.3 | async-start | bytes 1179648 | tf_op jit(solution)/shard_map/all_gather | solution.py:36
  7.9 462.7 %all-gather.5.cloned.1.call-start = ((), (), s32[]{:S(2)}) async-start(), calls=%async_computation.4 | async-start | bytes 21233664 | tf_op jit(solution)/shard_map/all_gather | solution.py:55
  375.1 3.8 copy-start.3
  375.1 3.8 copy-start.4
  388.8 110.2 %all-to-all-start.2 = ((bf16[32,2,24]{2,1,0:T(2,128)(2,1)}), bf16[32,2,24]{2,1,0:T(2,128)(2,1)S(1)}, u32[]{:S(2)}, u32[]{:S(2)}) async-start(bf16[32,2,24]{2,1,0:T(2,128)(2,1)} %broadcast_select_fusion), calls=%async_computation.2 | async-start | bytes 32768 | tf_op jit(solution)/shard_map/all_to_all | solution.py:46
  497.7 11.7 %copy-start.1 = (s32[128,8]{0,1:T(8,128)S(1)}, s32[128,8]{0,1:T(8,128)}, u32[]{:S(2)}) copy-start(s32[128,8]{0,1:T(8,128)} %param.9) | copy-start | bytes 12292
  497.7 11.7 %copy-start.2 = (f32[128,8]{0,1:T(8,128)S(1)}, f32[128,8]{0,1:T(8,128)}, u32[]{:S(2)}) copy-start(f32[128,8]{0,1:T(8,128)} %param.10) | copy-start | bytes 12292
  499.1 50.0 %all-to-all-start.1 = ((bf16[2,32,24,512]{3,2,0,1:T(8,128)(2,1)}), bf16[2,32,24,512]{3,2,0,1:T(8,128)(2,1)}, u32[]{:S(2)}, u32[]{:S(2)}) async-start(bf16[2,32,24,512]{3,2,0,1:T(8,128)(2,1)} %copy.46), calls=%async_computation.1 | async-start | bytes 3145728 | tf_op jit(solution)/shard_map/all_to_all | solution.py:59
Sparse Core Ops, SparseCore 0:
  9.8 28.8 all-gather.2
  379.0 91.6 all-gather.4
where the time goes:
time: 572 us; the launch traced here: 571 us
  blocking collectives  286 us (50%)
  waiting for transfers between devices  127 us (22%)
  local copies, waits for them, and re-layouts  71.1 us (12%)
  matrix products  30.7 us (5%)
  other arithmetic  25.9 us (5%)
  starting transfers between devices  15.8 us (3%)
  between operations  14.3 us (2%)
    all_to_all x1, blocking collectives, on_device(): lax.all_to_all(rows.reshape(owners, local_exp, capacity, whole.shape[1]),...  286 us
    all_gather x1, waiting for transfers between devices, on_device(): piece = lax.all_gather(hidden, 'col', axis=3, tiled=True)  76.2 us
    all_gather x1, waiting for transfers between devices, on_device(): whole = lax.all_gather(tokens, 'col', axis=1, tiled=True)  26.8 us
    all_to_all x1, waiting for transfers between devices, on_device(): lax.all_to_all(expert_out, 'expert', split_axis=1, concat_axis=0, tiled=T...  23.4 us
    gather x1, local copies, waits for them, and re-layouts, on_device(): rows = jnp.take(whole, flat_token, axis=0)  23.4 us
    all_gather x1, local copies, waits for them, and re-layouts, on_device(): piece = lax.all_gather(hidden, 'col', axis=3, tiled=True)  22.1 us
  transfers between devices with their start and end apart: 4, of which 3 were waited for; matrix products, arithmetic and copies ran while one was open for 10% of the time, Pallas kernels for 0%

commit v1 on v0

--- a/solution.py
+++ b/solution.py
@@ -52,7 +52,28 @@
         jnp.bfloat16
     )
     d_local = w_down.shape[2]
-    piece = lax.all_gather(hidden, "col", axis=3, tiled=True)
+    after, kept_arr, p_next = (lax.psum(1, "col"), lax.axis_index("col"), hidden.shape[3])
+    nodes = []
+    for h, k0 in enumerate(hidden.shape):
+        nodes.append(k0 * after if h == 3 else k0)
+    piece = lax.dynamic_update_slice_in_dim(
+        jnp.zeros(nodes, hidden.dtype), hidden, kept_arr * p_next, axis=3
+    )
+    z = back = hidden
+    for k in range(1, after // 2 + 1):
+        bank = []
+        for h in range(after):
+            bank.append((h, (h + 1) % after))
+        z = lax.ppermute(z, "col", bank)
+        piece = lax.dynamic_update_slice_in_dim(piece, z, (kept_arr - k) % after * p_next, axis=3)
+        if 2 * k < after:
+            rack = []
+            for h in range(after):
+                rack.append((h, (h - 1) % after))
+            back = lax.ppermute(back, "col", rack)
+            piece = lax.dynamic_update_slice_in_dim(
+                piece, back, (kept_arr + k) % after * p_next, axis=3
+            )
     block = jnp.einsum("escu,escv->euv", scaled, piece, preferred_element_type=jnp.float32)
     mixed_now = jnp.einsum("escv,evd->escd", piece, w_down, preferred_element_type=jnp.float32)
     expert_out = mixed_now.astype(jnp.bfloat16)

time: 572 us -> 600 us (1.049)
  local copies, waits for them, and re-layouts: 71.1 us -> 141 us
  waiting for transfers between devices: 127 us -> 75.6 us
  starting transfers between devices: 15.8 us -> 23.5 us
    dynamic_update_slice x0 -> x8, local copies, waits for them, and re-layouts: none -> 91 us  [the longest x4 45.1 us: on_device(): lax.dynamic_update_slice_in_dim(piece, z, (kept_arr - k) % after * p_next...]
    all_gather x1 -> x0, waiting for transfers between devices: 76.2 us -> none  [on_device(): piece = lax.all_gather(hidden, 'col', axis=3, tiled=True)]
    ppermute x0 -> x7, waiting for transfers between devices: none -> 29.2 us  [the longest x4 29.2 us: on_device(): z = lax.ppermute(z, 'col', bank)]
    all_gather x1 -> x0, local copies, waits for them, and re-layouts: 22.1 us -> none  [on_device(): piece = lax.all_gather(hidden, 'col', axis=3, tiled=True)]
    ppermute x0 -> x7, starting transfers between devices: none -> 8.02 us  [the longest x3 8.01 us: on_device(): back = lax.ppermute(back, 'col', rack)]
  transfers between devices with their start and end apart: 4 -> 10, of which waited for: 3 -> 5; matrix products, arithmetic and copies ran while one was open for 10% -> 22% of each run, Pallas kernels for 0% -> 0%
where the time goes in v1:
time: 600 us; the launch traced here: 597 us
  blocking collectives  286 us (48%)
  local copies, waits for them, and re-layouts  141 us (24%)
  waiting for transfers between devices  75.6 us (13%)
  matrix products  30.7 us (5%)
  other arithmetic  25.9 us (4%)
  starting transfers between devices  23.5 us (4%)
  between operations  14.4 us (2%)
    all_to_all x1, blocking collectives, on_device(): lax.all_to_all(rows.reshape(owners, local_exp, capacity, whole.shape[1]),...  286 us
    dynamic_update_slice x4, local copies, waits for them, and re-layouts, on_device(): lax.dynamic_update_slice_in_dim(piece, z, (kept_arr - k) % after * p_next...  45.1 us
    dynamic_update_slice x3, local copies, waits for them, and re-layouts, on_device(): lax.dynamic_update_slice_in_dim(piece, back, (kept_arr + k) % after * p_n...  37.1 us
    ppermute x4, waiting for transfers between devices, on_device(): z = lax.ppermute(z, 'col', bank)  29.2 us
    all_gather x1, waiting for transfers between devices, on_device(): whole = lax.all_gather(tokens, 'col', axis=1, tiled=True)  26.8 us
    gather x1, local copies, waits for them, and re-layouts, on_device(): rows = jnp.take(whole, flat_token, axis=0)  23.4 us
    all_to_all x1, waiting for transfers between devices, on_device(): lax.all_to_all(expert_out, 'expert', split_axis=1, concat_axis=0, tiled=T...  18.9 us
  transfers between devices with their start and end apart: 10, of which 5 were waited for; matrix products, arithmetic and copies ran while one was open for 22% of the time, Pallas kernels for 0%

profile of v1, /device:TPU:4, one launch (start us, length us, event | category | flops | bytes accessed | tf_op | source)
XLA Modules:
  0.0 596.6 jit_solution(10741539304051058633)
XLA Ops:
  11.9 26.8 %all-gather.2.cloned.1.call-done = bf16[128,4096]{1,0:T(8,128)(2,1)} async-done(((bf16[128,512]{1,0:T(8,128)(2,1)}), bf16[128,4096]{1,0:T(8,128)(2,1)}) %all-gather.2.cloned.1.call-update) | async-done | bytes 1048592 | tf_op jit(solution)/shard_map/all_gather | solution.py:36
  38.8 23.4 %gather_fusion = bf16[1536,4096]{1,0:T(8,128)(2,1)} fusion(bf16[128,4096]{1,0:T(8,128)(2,1)} %all-gather.2.cloned.1.call-done, s32[2048]{0:T(1024)S(1)} %pad_clamp_fusion.1), kind=kCustom, calls=%fused_computation | custom fusion | bytes 25171968 | tf_op jit(solution)/shard_map/jit(_take)/gather | solution.py:37
  62.2 6.7 %select_select_fusion = bf16[32,2,24,4096]{3,2,1,0:T(8,128)(2,1)S(1)} fusion(bf16[32,2,24,4096]{3,2,1,0:T(8,128)(2,1)} %bitcast.49, pred[32,2,24]{2,1,0:T(4,128)(4,1)S(1)} %compare_and_fusion, pred[32,2,24]{2,1,0:T(4,128)(4,1)S(1)} %broadcast_in_dim.99), kind=kLoop, calls=%fused_computation.4 | loop fusion | flops 12582912 | bytes 25168896 | tf_op jit(solution)/shard_map/jit(_where)/select_n | solution.py:38
  68.9 285.7 %all_to_all.19 = bf16[32,2,24,4096]{3,2,1,0:T(8,128)(2,1)} all-to-all(bf16[32,2,24,4096]{3,2,1,0:T(8,128)(2,1)S(1)} %select_select_fusion), channel_id=1, replica_groups=mesh['expert'=32,'col'=8] {'expert'}, dimensions={0} | all-to-all | bytes 25165824 | tf_op jit(solution)/shard_map/all_to_all | solution.py:39
  354.6 10.0 %fusion.2 = f32[2,32,24,192]{3,2,1,0:T(8,128)} fusion(bf16[32,2,24,4096]{3,2,1,0:T(8,128)(2,1)} %all_to_all.19, bf16[2,192,4096]{2,1,0:T(8,128)(2,1)} %param.13), kind=kOutput, calls=%fused_computation.7 | convolution fusion | flops 2415919104 | bytes 16908288 | tf_op jit(solution)/shard_map/seck,efk->escf/dot_general | solution.py:47
  364.7 10.5 %multiply_convert_fusion.1 = bf16[2,32,24,192]{3,2,1,0:T(8,128)(2,1)} fusion(f32[2,32,24,192]{3,2,1,0:T(8,128)} %fusion.2, bf16[2,192,4096]{2,1,0:T(8,128)(2,1)} %param.14, bf16[32,2,24,4096]{3,2,1,0:T(8,128)(2,1)} %all_to_all.19), kind=kOutput, calls=%fused_computation.18 | convolution fusion | flops 2417688576 | bytes 17498112 | tf_op jit(solution)/shard_map/seck,efk->escf/dot_general | solution.py:48
  378.2 9.9 %collective-permute-done = bf16[2,32,24,192]{3,2,1,0:T(8,128)(2,1)S(1)} collective-permute-done((bf16[2,32,24,192]{3,2,1,0:T(8,128)(2,1)}, bf16[2,32,24,192]{3,2,1,0:T(8,128)(2,1)S(1)}, u32[]{:S(2)}, u32[]{:S(2)}) %collective-permute-start) | collective-permute-done | bytes 589856 | tf_op jit(solution)/shard_map/ppermute | solution.py:67
  391.9 9.7 %collective-permute-done.2 = bf16[2,32,24,192]{3,2,1,0:T(8,128)(2,1)S(1)} collective-permute-done((bf16[2,32,24,192]{3,2,1,0:T(8,128)(2,1)S(1)}, bf16[2,32,24,192]{3,2,1,0:T(8,128)(2,1)S(1)}, u32[]{:S(2)}, u32[]{:S(2)}) %collective-permute-start.2) | collective-permute-done | bytes 589856 | tf_op jit(solution)/shard_map/ppermute | solution.py:67
  404.6 9.7 %collective-permute-done.4 = bf16[2,32,24,192]{3,2,1,0:T(8,128)(2,1)} collective-permute-done((bf16[2,32,24,192]{3,2,1,0:T(8,128)(2,1)S(1)}, bf16[2,32,24,192]{3,2,1,0:T(8,128)(2,1)}, u32[]{:S(2)}, u32[]{:S(2)}) %collective-permute-start.4) | collective-permute-done | bytes 589856 | tf_op jit(solution)/shard_map/ppermute | solution.py:67
  414.5 9.0 %gather_fusion.1 = bf16[1536]{0:T(1024)(128)(2,1)S(1)} fusion(bf16[128]{0:T(256)(128)(2,1)S(1)} %select_reduce_fusion.2, s32[2048]{0:T(1024)S(1)} %pad_clamp_fusion), kind=kCustom, calls=%fused_computation.1 | custom fusion | bytes 12288 | tf_op jit(solution)/shard_map/gather | solution.py:28
  424.3 5.6 all-to-all-start.2
  432.4 8.8 %dynamic_update_slice.24 = bf16[2,32,24,1536]{3,2,1,0:T(8,128)(2,1)} dynamic-update-slice(bf16[2,32,24,1536]{3,2,1,0:T(8,128)(2,1)} %broadcast_in_dim.98, bf16[2,32,24,192]{3,2,1,0:T(8,128)(2,1)} %multiply_convert_fusion.1, s32[]{:T(128)} %constant.90.clone.1, s32[]{:T(128)} %constant.90.clone.1, s32[]{:T(128)} %constant.90.clone.1, s32[]{:T(128)S(6)} %select_n.145) | dynamic-update-slice | bytes 1179652 | tf_op jit(solution)/shard_map/dynamic_update_slice | solution.py:59
  441.2 13.5 %dynamic_update_slice.25 = bf16[2,32,24,1536]{3,2,1,0:T(8,128)(2,1)} dynamic-update-slice(bf16[2,32,24,1536]{3,2,1,0:T(8,128)(2,1)} %dynamic_update_slice.24, bf16[2,32,24,192]{3,2,1,0:T(8,128)(2,1)} %copy-done.1, s32[]{:T(128)} %constant.90.clone.1, s32[]{:T(128)} %constant.90.clone.1, s32[]{:T(128)} %constant.90.clone.1, s32[]{:T(128)S(6)} %select_n.147) | dynamic-update-slice | bytes 1179652 | tf_op jit(solution)/shard_map/dynamic_update_slice | solution.py:68
  454.7 14.2 %dynamic_update_slice.26 = bf16[2,32,24,1536]{3,2,1,0:T(8,128)(2,1)} dynamic-update-slice(bf16[2,32,24,1536]{3,2,1,0:T(8,128)(2,1)} %dynamic_update_slice.25, bf16[2,32,24,192]{3,2,1,0:T(8,128)(2,1)} %copy-done.2, s32[]{:T(128)} %constant.90.clone.1, s32[]{:T(128)} %constant.90.clone.1, s32[]{:T(128)} %constant.90.clone.1, s32[]{:T(128)S(6)} %select_n.149) | dynamic-update-slice | bytes 1179652 | tf_op jit(solution)/shard_map/dynamic_update_slice | solution.py:74
  468.9 8.7 %dynamic_update_slice.27 = bf16[2,32,24,1536]{3,2,1,0:T(8,128)(2,1)} dynamic-update-slice(bf16[2,32,24,1536]{3,2,1,0:T(8,128)(2,1)} %dynamic_update_slice.26, bf16[2,32,24,192]{3,2,1,0:T(8,128)(2,1)} %copy-done.3, s32[]{:T(128)} %constant.90.clone.1, s32[]{:T(128)} %constant.90.clone.1, s32[]{:T(128)} %constant.90.clone.1, s32[]{:T(128)S(6)} %select_n.151) | dynamic-update-slice | bytes 1179652 | tf_op jit(solution)/shard_map/dynamic_update_slice | solution.py:68
  477.5 8.8 %dynamic_update_slice.28 = bf16[2,32,24,1536]{3,2,1,0:T(8,128)(2,1)} dynamic-update-slice(bf16[2,32,24,1536]{3,2,1,0:T(8,128)(2,1)} %dynamic_update_slice.27, bf16[2,32,24,192]{3,2,1,0:T(8,128)(2,1)} %collective-permute-done.3, s32[]{:T(128)} %constant.90.clone.1, s32[]{:T(128)} %constant.90.clone.1, s32[]{:T(128)} %constant.90.clone.1, s32[]{:T(128)S(6)} %select_n.153) | dynamic-update-slice | bytes 1179652 | tf_op jit(solution)/shard_map/dynamic_update_slice | solution.py:74
  486.3 14.1 %dynamic_update_slice.29 = bf16[2,32,24,1536]{3,2,1,0:T(8,128)(2,1)} dynamic-update-slice(bf16[2,32,24,1536]{3,2,1,0:T(8,128)(2,1)} %dynamic_update_slice.28, bf16[2,32,24,192]{3,2,1,0:T(8,128)(2,1)} %collective-permute-done.4, s32[]{:T(128)} %constant.90.clone.1, s32[]{:T(128)} %constant.90.clone.1, s32[]{:T(128)} %constant.90.clone.1, s32[]{:T(128)S(6)} %select_n.155) | dynamic-update-slice | bytes 1179652 | tf_op jit(solution)/shard_map/dynamic_update_slice | solution.py:68
  500.4 14.2 %dynamic_update_slice.30 = bf16[2,32,24,1536]{3,2,1,0:T(8,128)(2,1)} dynamic-update-slice(bf16[2,32,24,1536]{3,2,1,0:T(8,128)(2,1)} %dynamic_update_slice.29, bf16[2,32,24,192]{3,2,1,0:T(8,128)(2,1)} %collective-permute-done.5, s32[]{:T(128)} %constant.90.clone.1, s32[]{:T(128)} %constant.90.clone.1, s32[]{:T(128)} %constant.90.clone.1, s32[]{:T(128)S(6)} %select_n.157) | dynamic-update-slice | bytes 1179652 | tf_op jit(solution)/shard_map/dynamic_update_slice | solution.py:74
  514.6 8.8 %dynamic_update_slice.31 = bf16[2,32,24,1536]{3,2,1,0:T(8,128)(2,1)} dynamic-update-slice(bf16[2,32,24,1536]{3,2,1,0:T(8,128)(2,1)} %dynamic_update_slice.30, bf16[2,32,24,192]{3,2,1,0:T(8,128)(2,1)} %collective-permute-done.6, s32[]{:T(128)} %constant.90.clone.1, s32[]{:T(128)} %constant.90.clone.1, s32[]{:T(128)} %constant.90.clone.1, s32[]{:T(128)S(6)} %select_n.159) | dynamic-update-slice | bytes 1179652 | tf_op jit(solution)/shard_map/dynamic_update_slice | solution.py:68
  529.8 9.8 %all-to-all-start.1 = ((bf16[2,32,24,512]{3,2,0,1:T(8,128)(2,1)}), bf16[2,32,24,512]{3,2,0,1:T(8,128)(2,1)}, u32[]{:S(2)}, u32[]{:S(2)}) async-start(bf16[2,32,24,512]{3,2,0,1:T(8,128)(2,1)} %copy.57), calls=%async_computation.1 | async-start | bytes 3145728 | tf_op jit(solution)/shard_map/all_to_all | solution.py:80
  540.0 10.7 %gather_fusion.2 = f32[1536]{0:T(1024)S(1)} fusion(f32[64,128]{0,1:T(8,128)S(1)} %bitcast.48, s32[1536]{0:T(1024)S(1)} %reshape.137), kind=kCustom, calls=%fused_computation.2 | custom fusion | bytes 24576 | tf_op jit(solution)/shard_map/jit(take_along_axis)/gather | solution.py:32
  550.8 5.2 convolution_bitcast_fusion
  556.0 18.9 %all-to-all-done.1 = bf16[2,32,24,512]{3,2,0,1:T(8,128)(2,1)} async-done(((bf16[2,32,24,512]{3,2,0,1:T(8,128)(2,1)}), bf16[2,32,24,512]{3,2,0,1:T(8,128)(2,1)}, u32[]{:S(2)}, u32[]{:S(2)}) %all-to-all-start.1) | async-done | bytes 1572896 | tf_op jit(solution)/shard_map/all_to_all | solution.py:80
  578.6 10.4 %scatter_custom_fusion = f32[128,512]{1,0:T(8,128)S(1)} fusion(s32[1536]{0:T(1024)S(1)} %fusion.21, f32[1536,512]{1,0:T(8,128)} %bitcast_multiply_fusion, f32[]{:T(128)} %constant.87.clone.1), kind=kCustom, calls=%fused_computation.27 | custom fusion | flops 786432 | bytes 262656 | tf_op jit(solution)/shard_map/scatter-add | solution.py:83
  (64 shorter events, 29.1 us)
Async XLA Ops:
  7.2 516.2 %copy-start = (bf16[2,1536,512]{2,1,0:T(8,128)(2,1)S(1)}, bf16[2,1536,512]{2,1,0:T(8,128)(2,1)}, u32[]{:S(2)}) copy-start(bf16[2,1536,512]{2,1,0:T(8,128)(2,1)} %param.15) | copy-start | bytes 9437188
  7.2 31.6 %all-gather.2.cloned.1.call-start = ((), (), s32[]{:S(2)}) async-start(), calls=%async_computation.3 | async-start | bytes 1179648 | tf_op jit(solution)/shard_map/all_gather | solution.py:36
  364.7 49.7 %copy-start.6 = (f32[119]{0:T(128)S(1)}, f32[119]{0:T(128)}, u32[]{:S(2)}) copy-start(f32[119]{0:T(128)} %param.12) | copy-start | bytes 1432
  364.7 49.7 %copy-start.7 = (s32[128]{0:T(128)S(1)}, s32[128]{0:T(128)}, u32[]{:S(2)}) copy-start(s32[128]{0:T(128)} %param.11) | copy-start | bytes 1540
  375.2 12.8 %collective-permute-start = (bf16[2,32,24,192]{3,2,1,0:T(8,128)(2,1)}, bf16[2,32,24,192]{3,2,1,0:T(8,128)(2,1)S(1)}, u32[]{:S(2)}, u32[]{:S(2)}) collective-permute-start(bf16[2,32,24,192]{3,2,1,0:T(8,128)(2,1)} %multiply_convert_fusion.1), channel_id=1, source_target_pairs={{0,1},{1,2},{2,3},{3,4},{4,5},{5,6},{6,7},{7,0},{8,9},{9,10},{10,1... | collective-permute-start | bytes 1769480 | tf_op jit(solution)/shard_map/ppermute | solution.py:67
  375.2 13.7 %collective-permute-start.1 = (bf16[2,32,24,192]{3,2,1,0:T(8,128)(2,1)}, bf16[2,32,24,192]{3,2,1,0:T(8,128)(2,1)S(1)}, u32[]{:S(2)}, u32[]{:S(2)}) collective-permute-start(bf16[2,32,24,192]{3,2,1,0:T(8,128)(2,1)} %multiply_convert_fusion.1), channel_id=1, source_target_pairs={{0,7},{1,0},{2,1},{3,2},{4,3},{5,4},{6,5},{7,6},{8,15},{9,8},{10,9... | collective-permute-start | bytes 1769480 | tf_op jit(solution)/shard_map/ppermute | solution.py:73
  388.0 0.9 copy-start.1
  388.9 12.6 %collective-permute-start.2 = (bf16[2,32,24,192]{3,2,1,0:T(8,128)(2,1)S(1)}, bf16[2,32,24,192]{3,2,1,0:T(8,128)(2,1)S(1)}, u32[]{:S(2)}, u32[]{:S(2)}) collective-permute-start(bf16[2,32,24,192]{3,2,1,0:T(8,128)(2,1)S(1)} %collective-permute-done), channel_id=1, source_target_pairs={{0,1},{1,2},{2,3},{3,4},{4,5},{5,6},{6,7},{7,0},{8,9},{9,10},{10,1... | collective-permute-start | bytes 1769480 | tf_op jit(solution)/shard_map/ppermute | solution.py:67
  388.9 12.6 %copy-start.2 = (bf16[2,32,24,192]{3,2,1,0:T(8,128)(2,1)}, bf16[2,32,24,192]{3,2,1,0:T(8,128)(2,1)S(1)}, u32[]{:S(2)}) copy-start(bf16[2,32,24,192]{3,2,1,0:T(8,128)(2,1)S(1)} %collective-permute-done.1) | copy-start | bytes 1769476
  388.9 12.6 %collective-permute-start.3 = (bf16[2,32,24,192]{3,2,1,0:T(8,128)(2,1)S(1)}, bf16[2,32,24,192]{3,2,1,0:T(8,128)(2,1)}, u32[]{:S(2)}, u32[]{:S(2)}) collective-permute-start(bf16[2,32,24,192]{3,2,1,0:T(8,128)(2,1)S(1)} %collective-permute-done.1), channel_id=1, source_target_pairs={{0,7},{1,0},{2,1},{3,2},{4,3},{5,4},{6,5},{7,6},{8,15},{9,8},{10,9... | collective-permute-start | bytes 1769480 | tf_op jit(solution)/shard_map/ppermute | solution.py:73
  401.5 1.0 copy-start.3
  401.5 12.7 %collective-permute-start.4 = (bf16[2,32,24,192]{3,2,1,0:T(8,128)(2,1)S(1)}, bf16[2,32,24,192]{3,2,1,0:T(8,128)(2,1)}, u32[]{:S(2)}, u32[]{:S(2)}) collective-permute-start(bf16[2,32,24,192]{3,2,1,0:T(8,128)(2,1)S(1)} %collective-permute-done.2), channel_id=1, source_target_pairs={{0,1},{1,2},{2,3},{3,4},{4,5},{5,6},{6,7},{7,0},{8,9},{9,10},{10,1... | collective-permute-start | bytes 1769480 | tf_op jit(solution)/shard_map/ppermute | solution.py:67
  402.5 97.9 %collective-permute-start.5 = (bf16[2,32,24,192]{3,2,1,0:T(8,128)(2,1)}, bf16[2,32,24,192]{3,2,1,0:T(8,128)(2,1)}, u32[]{:S(2)}, u32[]{:S(2)}) collective-permute-start(bf16[2,32,24,192]{3,2,1,0:T(8,128)(2,1)} %collective-permute-done.3), channel_id=1, source_target_pairs={{0,7},{1,0},{2,1},{3,2},{4,3},{5,4},{6,5},{7,6},{8,15},{9,8},{10,9... | collective-permute-start | bytes 1769480 | tf_op jit(solution)/shard_map/ppermute | solution.py:73
  414.3 100.3 %collective-permute-start.6 = (bf16[2,32,24,192]{3,2,1,0:T(8,128)(2,1)}, bf16[2,32,24,192]{3,2,1,0:T(8,128)(2,1)}, u32[]{:S(2)}, u32[]{:S(2)}) collective-permute-start(bf16[2,32,24,192]{3,2,1,0:T(8,128)(2,1)} %collective-permute-done.4), channel_id=1, source_target_pairs={{0,1},{1,2},{2,3},{3,4},{4,5},{5,6},{6,7},{7,0},{8,9},{9,10},{10,1... | collective-permute-start | bytes 1769480 | tf_op jit(solution)/shard_map/ppermute | solution.py:67
  424.3 105.5 %all-to-all-start.2 = ((bf16[32,2,24]{2,1,0:T(2,128)(2,1)}), bf16[32,2,24]{2,1,0:T(2,128)(2,1)S(1)}, u32[]{:S(2)}, u32[]{:S(2)}) async-start(bf16[32,2,24]{2,1,0:T(2,128)(2,1)} %broadcast_select_fusion), calls=%async_computation.2 | async-start | bytes 32768 | tf_op jit(solution)/shard_map/all_to_all | solution.py:46
  528.4 11.5 %copy-start.4 = (s32[128,8]{0,1:T(8,128)S(1)}, s32[128,8]{0,1:T(8,128)}, u32[]{:S(2)}) copy-start(s32[128,8]{0,1:T(8,128)} %param.9) | copy-start | bytes 12292
  528.4 11.5 %copy-start.5 = (f32[128,8]{0,1:T(8,128)S(1)}, f32[128,8]{0,1:T(8,128)}, u32[]{:S(2)}) copy-start(f32[128,8]{0,1:T(8,128)} %param.10) | copy-start | bytes 12292
  529.8 45.1 %all-to-all-start.1 = ((bf16[2,32,24,512]{3,2,0,1:T(8,128)(2,1)}), bf16[2,32,24,512]{3,2,0,1:T(8,128)(2,1)}, u32[]{:S(2)}, u32[]{:S(2)}) async-start(bf16[2,32,24,512]{3,2,0,1:T(8,128)(2,1)} %copy.57), calls=%async_computation.1 | async-start | bytes 3145728 | tf_op jit(solution)/shard_map/all_to_all | solution.py:80
Sparse Core Ops, SparseCore 0:
  9.8 28.8 all-gather.1
